TPU v7x, 128 devices: a whole 4x4x4 slice. The times are simulated.
128 devices in a mesh: tu: 16 (over x, z), tv: 8 (over y, core).
Axes of the slice: x: 4, y: 4, z: 4, core: 2. Of those that a mesh axis runs over, the one named last changes fastest.
Arguments:
- aperture_amp: bfloat16 [512, 512, 512], P(('tu', 'tv')), may hold values from 0.19921875 to 1.796875
- aperture_phase: bfloat16 [512, 512, 512], P(('tu', 'tv')), may hold values from -3.140625 to 3.140625
- plane_depths: float32 [4], replicated, may hold values from 8 to 344
- send_list: int32 [128, 128, 2], P(('tu', 'tv')), may hold values from 0 to 15, as said below
- send_count: int32 [128, 128], P(('tu', 'tv')), may hold values from 0 to 2, as said below
- vis_left: bfloat16 [49152, 128, 128], P(('tu', 'tv')), may hold values from -0.078125 to 0.078125
- vis_right: bfloat16 [49152, 64, 128], P(('tu', 'tv')), may hold values from -0.75 to 0.75
- block_slot: int32 [49152], P(('tu', 'tv')), may hold values from 0 to 255, as said below
- block_pos: int32 [49152], P(('tu', 'tv')), may hold values from 0 to 31
- block_count: int32 [128], P(('tu', 'tv')), may hold values from 96 to 384, as said below
Outputs:
- uv_grid: float32 [2, 4096, 4096], P(None, 'tu', 'tv')
Inputs may be any that keep to these rules, and one draw needn't show every extreme that they name: `send_list`: each owner sends every one of its kernels to 8 slots, 128 in all; the used slots of an owner and tile are the first send_count of them; entries of unused slots are arbitrary kernel numbers in range. One tile, drawn afresh, receives 2 slots from every owner; a row of send_count sums to 128. `block_slot`: names a slot r = d * 2 + c that the block's tile receives, with c < send_count[d, tile]. `block_count`: some tile uses all 384 slots.
All inputs are finite; a program needn't handle non-finite values.
Results may differ from a plain program's by a relative error of at most 0.0065.
Values may be sent and summed in bfloat16 or wider, within the bound.
A program may use at most 192 MiB of HBM per device.

v0:
```python
import math

import jax
import jax.numpy as jnp
from jax import lax
from jax.sharding import PartitionSpec as P

KSIZE = 64
TILE_U = 256
TILE_V = 512


def from_behind(block, axis, distance):
    devices = range(lax.axis_size(axis))
    route = [(i - distance, i) for i in devices if i - distance in devices]
    return lax.ppermute(block, axis, route)


def dft_table(kernel_size, screen_size):
    frequency = jnp.arange(kernel_size, dtype=jnp.int32) - kernel_size // 2
    cell_ids = jnp.arange(screen_size, dtype=jnp.int32)
    turns = jnp.mod(frequency[:, None] * cell_ids[None, :], screen_size).astype(jnp.float32)
    angles = 2.0 * math.pi / screen_size * turns
    return jnp.concatenate([jnp.cos(angles), -jnp.sin(angles)], axis=0).astype(jnp.bfloat16)


def aperture_screens(amplitude, phase_rows, plane_depths):
    screen_size = amplitude.shape[-1]
    coords = (
        jnp.arange(screen_size, dtype=jnp.int32).astype(jnp.float32) - screen_size // 2
    ) / screen_size
    radius = coords[:, None] ** 2 + coords[None, :] ** 2
    angles = (
        phase_rows.astype(jnp.float32)[:, None]
        + 2.0 * math.pi * plane_depths[None, :, None, None] * radius
    )
    magnitude = amplitude.astype(jnp.float32)[:, None]
    real_part = (magnitude * jnp.cos(angles)).astype(jnp.bfloat16)
    imag_part = (magnitude * jnp.sin(angles)).astype(jnp.bfloat16)
    stacked = jnp.concatenate([real_part, imag_part], axis=-1)
    return stacked.reshape(-1, screen_size, 2 * screen_size)


def kernels_from(stacked, kernel_size):
    screen_size = stacked.shape[1]
    dft = dft_table(kernel_size, screen_size)
    product = jnp.einsum("as,ksn->kan", dft, stacked, preferred_element_type=jnp.float32)
    half_real = product[:, :kernel_size, :screen_size] - product[:, kernel_size:, screen_size:]
    half_imag = product[:, :kernel_size, screen_size:] + product[:, kernel_size:, :screen_size]
    halves = jnp.concatenate([half_real, half_imag], axis=1).astype(jnp.bfloat16)
    second = jnp.einsum("kas,bs->kab", halves, dft, preferred_element_type=jnp.float32)
    out_real = second[:, :kernel_size, :kernel_size] - second[:, kernel_size:, kernel_size:]
    out_imag = second[:, :kernel_size, kernel_size:] + second[:, kernel_size:, :kernel_size]
    return (jnp.concatenate([out_real, out_imag], axis=-1) / screen_size).astype(jnp.bfloat16)


def grid_patches(block_kernels, left_rows, right_rows):
    kernel_size = block_kernels.shape[1]
    real_k = block_kernels[:, :, :kernel_size]
    imag_k = block_kernels[:, :, kernel_size:]
    operator_rows = jnp.concatenate(
        [block_kernels, jnp.concatenate([-imag_k, real_k], axis=2)], axis=1
    )
    mixed = jnp.einsum(
        "gpc,gcd->gpd", left_rows, operator_rows, preferred_element_type=jnp.float32
    ).astype(jnp.bfloat16)
    stacked_rows = mixed.reshape(mixed.shape[0], 2 * mixed.shape[1], kernel_size)
    return jnp.einsum("grk,gkq->grq", stacked_rows, right_rows, preferred_element_type=jnp.float32)


def split_groups(values, group_count):
    return values.reshape((group_count, values.shape[0] // group_count) + values.shape[1:])


def shards(
    aperture_amp,
    aperture_phase,
    plane_depths,
    send_list,
    send_count,
    vis_left,
    vis_right,
    block_slot,
    block_pos,
    block_count,
):
    kernels = kernels_from(aperture_screens(aperture_amp, aperture_phase, plane_depths), KSIZE)
    send_rows = send_list[0]
    counts = send_count[0]
    capacity = send_rows.shape[1]
    is_live = jnp.arange(capacity, dtype=jnp.int32)[None, :] < counts[:, None]
    outgoing = jnp.where(is_live[:, :, None, None], kernels[send_rows], jnp.zeros((), jnp.bfloat16))
    arrived = lax.all_to_all(outgoing, ("tu", "tv"), split_axis=0, concat_axis=0, tiled=True)
    received = arrived.reshape(-1, KSIZE, 2 * KSIZE)
    block_total = vis_left.shape[0]
    group_size = min(128, block_total)
    group_count = block_total // group_size
    row_slots = TILE_U // KSIZE
    col_slots = TILE_V // KSIZE
    ext_cols = col_slots + 1
    ext_total = (row_slots + 1) * ext_cols
    block_ids = jnp.arange(block_total, dtype=jnp.int32)
    targets = jnp.arange(ext_total, dtype=jnp.int32)
    tile_count = block_count[0]

    def grid_group(placed, grouped):
        left_rows, right_rows, slot_ids, positions, member_ids = grouped
        patches = grid_patches(received[slot_ids], left_rows, right_rows)
        quarters = patches.reshape(group_size, 2, KSIZE, 2, 2, KSIZE)
        row_anchor = positions // col_slots
        col_anchor = positions % col_slots
        member_live = member_ids < tile_count
        for row_half in range(2):
            for col_half in range(2):
                dest = (row_anchor + row_half) * ext_cols + col_anchor + col_half
                onehot = ((dest[None, :] == targets[:, None]) & member_live[None, :]).astype(
                    jnp.float32
                )
                piece = quarters[:, row_half, :, :, col_half, :].reshape(group_size, -1)
                placed = placed + jnp.dot(onehot, piece, precision=lax.Precision.HIGHEST)
        return (placed, None)

    grouped = (
        split_groups(vis_left, group_count),
        split_groups(vis_right, group_count),
        split_groups(block_slot, group_count),
        split_groups(block_pos, group_count),
        split_groups(block_ids, group_count),
    )
    start = jnp.zeros((ext_total, 2 * KSIZE * KSIZE), jnp.float32)
    placed, unused = lax.scan(grid_group, start, grouped)
    extended = placed.reshape(row_slots + 1, ext_cols, KSIZE, 2, KSIZE).transpose(3, 0, 2, 1, 4)
    extended = extended.reshape(2, (row_slots + 1) * KSIZE, ext_cols * KSIZE)
    bottom = extended[:, TILE_U:, :]
    arrived_rows = from_behind(bottom.astype(jnp.bfloat16), "tu", 1).astype(bottom.dtype)
    extended = extended.at[:, :KSIZE, :].add(arrived_rows)
    side = extended[:, :TILE_U, TILE_V:]
    arrived_cols = from_behind(side.astype(jnp.bfloat16), "tv", 1).astype(side.dtype)
    result = extended[:, :TILE_U, :TILE_V].at[:, :, :KSIZE].add(arrived_cols)
    return result


def solution(mesh):
    placed = (
        P(("tu", "tv"), None, None),
        P(("tu", "tv"), None, None),
        P(),
        P(("tu", "tv"), None, None),
        P(("tu", "tv"), None),
        P(("tu", "tv"), None, None),
        P(("tu", "tv"), None, None),
        P(("tu", "tv")),
        P(("tu", "tv")),
        P(("tu", "tv")),
    )
    return jax.shard_map(
        shards, mesh=mesh, in_specs=placed, out_specs=P(None, "tu", "tv"), check_vma=False
    )
```

profile of v0, /device:TPU:0, one launch (start us, length us, event | category | flops | bytes accessed | tf_op | source)
XLA Modules:
  0.0 424.0 jit_solution(10817195657862718123)
XLA Ops:
  0.8 0.7 broadcast_multiply_fusion.1
  1.4 2.2 convert_element_type.59
  4.2 0.7 broadcast_multiply_fusion
  4.9 61.6 %fusion.42 = (bf16[4,4,512,512]{3,2,1,0:T(8,128)(2,1)S(1)}, bf16[4,4,512,512]{3,2,1,0:T(8,128)(2,1)}) fusion(f32[4,512,512]{2,1,0:T(8,128)S(1)} %broadcast_multiply_fusion, f32[4,512,512]{2,1,0:T(8,128)S(1)} %convert_element_type.60, f32[4,512,512]{2,1,0:T(8,128)S(1)} %convert_element_type.59), kind=kLoop, calls=%fused_computation.61 | loop fusion | flops 20971520 | bytes 29360128 | tf_op jit(solution)/shard_map/convert_element_type | solution.py:38
  66.5 6.7 %fusion.49 = f32[16,128,1024]{2,1,0:T(8,128)} fusion(bf16[16,512,512]{2,1,0:T(8,128)(2,1)} %bitcast.106, bf16[16,512,512]{2,1,0:T(8,128)(2,1)S(1)} %bitcast.105, bf16[64,512]{1,0:T(8,128)(2,1)S(1)} %get-tuple-element.262, bf16[64,512]{1,0:T(8,128)(2,1)S(1)} %get-tuple-element.261), kind=kOutput, calls=%fused_computation.69 | convolution fusion | flops 2181300224 | bytes 25296896 | tf_op jit(solution)/shard_map/as,ksn->kan/dot_general | solution.py:47
  73.2 4.3 %fusion.53 = (bf16[16,64,512]{2,1,0:T(8,128)(2,1)S(1)}, bf16[16,64,512]{2,1,0:T(8,128)(2,1)S(1)}) fusion(f32[16,128,1024]{2,1,0:T(8,128)} %fusion.49), kind=kLoop, calls=%fused_computation.73 | loop fusion | flops 2097152 | bytes 10485760 | tf_op jit(solution)/shard_map/convert.2
  77.5 0.7 fusion.54
  79.1 3.1 gather_fusion.1
  82.2 3.8 broadcast_select_fusion
  86.0 11.7 %all-to-all-start = ((bf16[128,2,64,128]{3,2,1,0:T(8,128)(2,1)}), bf16[128,2,64,128]{3,2,1,0:T(8,128)(2,1)}, u32[]{:S(2)}, u32[]{:S(2)}) async-start(bf16[128,2,64,128]{3,2,1,0:T(8,128)(2,1)} %broadcast_select_fusion), calls=%async_computation | async-start | bytes 8388608 | tf_op jit(solution)/shard_map/all_to_all | solution.py:93
  97.7 52.5 %all-to-all-done = bf16[128,2,64,128]{3,2,1,0:T(8,128)(2,1)} async-done(((bf16[128,2,64,128]{3,2,1,0:T(8,128)(2,1)}), bf16[128,2,64,128]{3,2,1,0:T(8,128)(2,1)}, u32[]{:S(2)}, u32[]{:S(2)}) %all-to-all-start) | async-done | bytes 4194336 | tf_op jit(solution)/shard_map/all_to_all | solution.py:93
  150.3 243.2 %while.16 = (s32[]{:T(128)}, f32[45,8192]{1,0:T(8,128)}, s32[3,128]{1,0:T(4,128)}, s32[3,128]{1,0:T(4,128)S(1)}, s32[]{:T(128)}, /*index=5*/bf16[3,128,128,128]{...) while((s32[]{:T(128)}, f32[45,8192]{1,0:T(8,128)}, ...), condition=%wide.region_1.2_spmd.clone.clone, body=%wide.region_0.1_spmd.clone.clone.sunk | while | flops 3355764736 | bytes 212745104 | solution.py:131
  150.3 0.7 fusion.103
  151.0 3.1 gather_fusion
  154.1 0.9 slice_negate_fusion.2
  155.0 5.7 %fusion.104 = bf16[128,128,128]{2,1,0:T(8,128)(2,1)} fusion(bf16[128,64,64]{2,1,0:T(8,128)(2,1)S(1)} %get-tuple-element.330, bf16[128,64,64]{2,1,0:T(8,128)(2,1)S(1)} %get-tuple-element.331, bf16[128,64,128]{2,1,0:T(8,128)(2,1)S(1)} %gather_fusion, bf16[3,128,128,128]{3,2,1,0:T(8,128)(2,1)} %get-tuple-element.369, s32[]{:T(128)} %get-tuple-element.353), kind=kOutput, calls=%fused_computation.15.clone.1 | convolution fusion | flops 551550976 | bytes 12583424 | tf_op jit(solution)/shard_map/while/body/eval_jaxpr/gpc,gcd->gpd/dot_general | solution.py:64
  160.7 6.9 %copy.22 = bf16[128,128,128]{0,2,1:T(8,128)(2,1)} copy(bf16[128,128,128]{2,1,0:T(8,128)(2,1)} %fusion.104) | data formatting | bytes 8388608 | tf_op jit(solution)/shard_map/while/body/eval_jaxpr/convert_element_type | solution.py:66
  167.6 7.4 %copy.23 = bf16[128,256,64]{1,2,0:T(8,128)(2,1)} copy(bf16[128,256,64]{0,2,1:T(8,128)(2,1)} %bitcast.97) | data formatting | bytes 8388608 | tf_op jit(solution)/shard_map/while/body/eval_jaxpr/reshape | solution.py:67
  175.0 11.0 %fusion.105 = f32[128,256,128]{2,1,0:T(8,128)} fusion(bf16[128,256,64]{1,2,0:T(8,128)(2,1)} %copy.23, bf16[3,128,64,128]{3,2,1,0:T(8,128)(2,1)} %get-tuple-element.372, s32[]{:T(128)} %get-tuple-element.353), kind=kOutput, calls=%fused_computation.17.clone.1 | convolution fusion | flops 536870912 | bytes 23069184 | tf_op jit(solution)/shard_map/while/body/eval_jaxpr/grk,gkq->grq/dot_general | solution.py:68
  186.0 17.6 %copy.24 = f32[128,256,128]{0,2,1:T(8,128)} copy(f32[128,256,128]{2,1,0:T(8,128)} %fusion.105) | data formatting | bytes 33554432 | tf_op jit(solution)/shard_map/while/body/eval_jaxpr/grk,gkq->grq/dot_general | solution.py:68
  203.6 12.6 %fusion.106 = (f32[128,1,64,2,1,64]{0,5,4,3,2,1:T(8,128)}, f32[128,1,64,2,1,64]{0,5,4,3,2,1:T(8,128)}, f32[128,1,64,2,1,64]{0,5,4,3,2,1:T(8,128)}, f32[128,1,64,2,1,64]{0,5,4,3,2,1:T(8,128)}) fusion(f32[128,2,64,2,2,64]{0,5,4,3,2,1:T(8,128)} %bitcast.96), kind=kLoop, calls=%fused_computation.110.clone.1 | loop fusion | bytes 33554432 | tf_op jit(solution)/shard_map/while/body/eval_jaxpr/slice | solution.py:119
  216.1 0.7 add_bitcast_fusion.3
  216.8 0.7 compare_bitcast_fusion.2
  217.5 4.8 %convolution_add_fusion.8 = f32[45,8192]{1,0:T(8,128)S(1)} fusion(f32[128,8192]{0,1:T(8,128)} %bitcast.101, f32[45,8192]{1,0:T(8,128)S(1)} %copy-done.3, pred[]{:T(512)S(6)} %compare.37, s32[128]{0:T(128)S(1)} %get-tuple-element.335, pred[128]{0:T(512)(128)(4,1)S(1)} %compare_bitcast_fusion.2), kind=kOutput, calls=%fused_computation.6.clone.1 | convolution fusion | flops 566979840 | bytes 7144065 | tf_op jit(solution)/shard_map/while/body/eval_jaxpr/dot_general | solution.py:120
  222.4 2.6 convolution_add_fusion.9
  225.0 2.6 convolution_add_fusion.10
  227.6 3.7 convolution_add_fusion.11
  231.3 0.7 fusion.103
  232.0 3.1 gather_fusion
  235.2 0.9 slice_negate_fusion.2
  236.1 5.7 %fusion.104 = bf16[128,128,128]{2,1,0:T(8,128)(2,1)} fusion(bf16[128,64,64]{2,1,0:T(8,128)(2,1)S(1)} %get-tuple-element.330, bf16[128,64,64]{2,1,0:T(8,128)(2,1)S(1)} %get-tuple-element.331, bf16[128,64,128]{2,1,0:T(8,128)(2,1)S(1)} %gather_fusion, bf16[3,128,128,128]{3,2,1,0:T(8,128)(2,1)} %get-tuple-element.369, s32[]{:T(128)} %get-tuple-element.353), kind=kOutput, calls=%fused_computation.15.clone.1 | convolution fusion | flops 551550976 | bytes 12583424 | tf_op jit(solution)/shard_map/while/body/eval_jaxpr/gpc,gcd->gpd/dot_general | solution.py:64
  241.8 6.9 %copy.22 = bf16[128,128,128]{0,2,1:T(8,128)(2,1)} copy(bf16[128,128,128]{2,1,0:T(8,128)(2,1)} %fusion.104) | data formatting | bytes 8388608 | tf_op jit(solution)/shard_map/while/body/eval_jaxpr/convert_element_type | solution.py:66
  248.6 7.4 %copy.23 = bf16[128,256,64]{1,2,0:T(8,128)(2,1)} copy(bf16[128,256,64]{0,2,1:T(8,128)(2,1)} %bitcast.97) | data formatting | bytes 8388608 | tf_op jit(solution)/shard_map/while/body/eval_jaxpr/reshape | solution.py:67
  256.0 11.0 %fusion.105 = f32[128,256,128]{2,1,0:T(8,128)} fusion(bf16[128,256,64]{1,2,0:T(8,128)(2,1)} %copy.23, bf16[3,128,64,128]{3,2,1,0:T(8,128)(2,1)} %get-tuple-element.372, s32[]{:T(128)} %get-tuple-element.353), kind=kOutput, calls=%fused_computation.17.clone.1 | convolution fusion | flops 536870912 | bytes 23069184 | tf_op jit(solution)/shard_map/while/body/eval_jaxpr/grk,gkq->grq/dot_general | solution.py:68
  267.0 17.6 %copy.24 = f32[128,256,128]{0,2,1:T(8,128)} copy(f32[128,256,128]{2,1,0:T(8,128)} %fusion.105) | data formatting | bytes 33554432 | tf_op jit(solution)/shard_map/while/body/eval_jaxpr/grk,gkq->grq/dot_general | solution.py:68
  284.6 12.6 %fusion.106 = (f32[128,1,64,2,1,64]{0,5,4,3,2,1:T(8,128)}, f32[128,1,64,2,1,64]{0,5,4,3,2,1:T(8,128)}, f32[128,1,64,2,1,64]{0,5,4,3,2,1:T(8,128)}, f32[128,1,64,2,1,64]{0,5,4,3,2,1:T(8,128)}) fusion(f32[128,2,64,2,2,64]{0,5,4,3,2,1:T(8,128)} %bitcast.96), kind=kLoop, calls=%fused_computation.110.clone.1 | loop fusion | bytes 33554432 | tf_op jit(solution)/shard_map/while/body/eval_jaxpr/slice | solution.py:119
  297.2 0.7 add_bitcast_fusion.3
  298.6 4.9 %convolution_add_fusion.8 = f32[45,8192]{1,0:T(8,128)S(1)} fusion(f32[128,8192]{0,1:T(8,128)} %bitcast.101, f32[45,8192]{1,0:T(8,128)S(1)} %copy-done.3, pred[]{:T(512)S(6)} %compare.37, s32[128]{0:T(128)S(1)} %get-tuple-element.335, pred[128]{0:T(512)(128)(4,1)S(1)} %compare_bitcast_fusion.2), kind=kOutput, calls=%fused_computation.6.clone.1 | convolution fusion | flops 566979840 | bytes 7144065 | tf_op jit(solution)/shard_map/while/body/eval_jaxpr/dot_general | solution.py:120
  303.5 2.6 convolution_add_fusion.9
  306.1 2.6 convolution_add_fusion.10
  308.7 3.7 convolution_add_fusion.11
  312.4 0.7 fusion.103
  313.1 3.1 gather_fusion
  316.2 0.9 slice_negate_fusion.2
  317.1 5.7 %fusion.104 = bf16[128,128,128]{2,1,0:T(8,128)(2,1)} fusion(bf16[128,64,64]{2,1,0:T(8,128)(2,1)S(1)} %get-tuple-element.330, bf16[128,64,64]{2,1,0:T(8,128)(2,1)S(1)} %get-tuple-element.331, bf16[128,64,128]{2,1,0:T(8,128)(2,1)S(1)} %gather_fusion, bf16[3,128,128,128]{3,2,1,0:T(8,128)(2,1)} %get-tuple-element.369, s32[]{:T(128)} %get-tuple-element.353), kind=kOutput, calls=%fused_computation.15.clone.1 | convolution fusion | flops 551550976 | bytes 12583424 | tf_op jit(solution)/shard_map/while/body/eval_jaxpr/gpc,gcd->gpd/dot_general | solution.py:64
  322.8 6.9 %copy.22 = bf16[128,128,128]{0,2,1:T(8,128)(2,1)} copy(bf16[128,128,128]{2,1,0:T(8,128)(2,1)} %fusion.104) | data formatting | bytes 8388608 | tf_op jit(solution)/shard_map/while/body/eval_jaxpr/convert_element_type | solution.py:66
  329.7 7.4 %copy.23 = bf16[128,256,64]{1,2,0:T(8,128)(2,1)} copy(bf16[128,256,64]{0,2,1:T(8,128)(2,1)} %bitcast.97) | data formatting | bytes 8388608 | tf_op jit(solution)/shard_map/while/body/eval_jaxpr/reshape | solution.py:67
  337.1 11.0 %fusion.105 = f32[128,256,128]{2,1,0:T(8,128)} fusion(bf16[128,256,64]{1,2,0:T(8,128)(2,1)} %copy.23, bf16[3,128,64,128]{3,2,1,0:T(8,128)(2,1)} %get-tuple-element.372, s32[]{:T(128)} %get-tuple-element.353), kind=kOutput, calls=%fused_computation.17.clone.1 | convolution fusion | flops 536870912 | bytes 23069184 | tf_op jit(solution)/shard_map/while/body/eval_jaxpr/grk,gkq->grq/dot_general | solution.py:68
  348.1 17.6 %copy.24 = f32[128,256,128]{0,2,1:T(8,128)} copy(f32[128,256,128]{2,1,0:T(8,128)} %fusion.105) | data formatting | bytes 33554432 | tf_op jit(solution)/shard_map/while/body/eval_jaxpr/grk,gkq->grq/dot_general | solution.py:68
  365.7 12.6 %fusion.106 = (f32[128,1,64,2,1,64]{0,5,4,3,2,1:T(8,128)}, f32[128,1,64,2,1,64]{0,5,4,3,2,1:T(8,128)}, f32[128,1,64,2,1,64]{0,5,4,3,2,1:T(8,128)}, f32[128,1,64,2,1,64]{0,5,4,3,2,1:T(8,128)}) fusion(f32[128,2,64,2,2,64]{0,5,4,3,2,1:T(8,128)} %bitcast.96), kind=kLoop, calls=%fused_computation.110.clone.1 | loop fusion | bytes 33554432 | tf_op jit(solution)/shard_map/while/body/eval_jaxpr/slice | solution.py:119
  378.3 0.7 add_bitcast_fusion.3
  379.7 4.9 %convolution_add_fusion.8 = f32[45,8192]{1,0:T(8,128)S(1)} fusion(f32[128,8192]{0,1:T(8,128)} %bitcast.101, f32[45,8192]{1,0:T(8,128)S(1)} %copy-done.3, pred[]{:T(512)S(6)} %compare.37, s32[128]{0:T(128)S(1)} %get-tuple-element.335, pred[128]{0:T(512)(128)(4,1)S(1)} %compare_bitcast_fusion.2), kind=kOutput, calls=%fused_computation.6.clone.1 | convolution fusion | flops 566979840 | bytes 7144065 | tf_op jit(solution)/shard_map/while/body/eval_jaxpr/dot_general | solution.py:120
  384.5 2.6 convolution_add_fusion.9
  387.1 2.6 convolution_add_fusion.10
  389.8 3.7 convolution_add_fusion.11
  393.5 3.4 reshape.270
  396.9 5.1 %copy.17 = f32[5,9,64,2,64]{2,0,4,1,3:T(8,128)} copy(f32[5,9,64,2,64]{4,3,2,1,0:T(2,128)S(1)} %reshape.270) | data formatting | bytes 2949120 | tf_op jit(solution)/shard_map/reshape | solution.py:132
  402.0 3.5 reshape.271
  405.6 2.5 collective-permute-start
  408.0 5.1 %collective-permute-done = bf16[2,64,576]{1,2,0:T(8,128)(2,1)S(1)} collective-permute-done((bf16[2,64,576]{1,2,0:T(8,128)(2,1)S(1)}, bf16[2,64,576]{1,2,0:T(8,128)(2,1)S(1)}, u32[]{:S(2)}, u32[]{:S(2)}) %collective-permute-start) | collective-permute-done | bytes 147488 | tf_op jit(solution)/shard_map/ppermute | solution.py:16
  413.2 7.2 %scatter-add.6 = f32[2,320,576]{1,2,0:T(8,128)S(1)} dynamic-update-slice(f32[2,320,576]{1,2,0:T(8,128)S(1)} %reshape.271, f32[2,64,576]{1,2,0:T(8,128)S(1)} %slice_add_fusion.1, s32[]{:T(128)} %constant.151.clone.1, s32[]{:T(128)} %constant.151.clone.1, s32[]{:T(128)} %constant.151.clone.1) | dynamic-update-slice | bytes 589828 | tf_op jit(solution)/shard_map/scatter-add | solution.py:136
  420.4 1.3 collective-permute-start.1
  421.8 0.8 collective-permute-done.1
  422.6 1.3 copy.18
  (57 shorter events, 3.8 us)
Async XLA Ops:
  0.0 3.6 copy-start.4
  77.5 1.1 copy-start.5
  77.5 1.4 copy-start.6
  86.0 64.3 %all-to-all-start = ((bf16[128,2,64,128]{3,2,1,0:T(8,128)(2,1)}), bf16[128,2,64,128]{3,2,1,0:T(8,128)(2,1)}, u32[]{:S(2)}, u32[]{:S(2)}) async-start(bf16[128,2,64,128]{3,2,1,0:T(8,128)(2,1)} %broadcast_select_fusion), calls=%async_computation | async-start | bytes 8388608 | tf_op jit(solution)/shard_map/all_to_all | solution.py:93
  203.6 14.0 %copy-start.3 = (f32[45,8192]{1,0:T(8,128)S(1)}, f32[45,8192]{1,0:T(8,128)}, u32[]{:S(2)}) copy-start(f32[45,8192]{1,0:T(8,128)} %get-tuple-element.354) | copy-start | bytes 4423684 | tf_op jit(solution)/shard_map/while
  217.5 4.9 %copy-start.2 = (f32[128,1,64,2,1,64]{0,5,4,3,2,1:T(8,128)S(1)}, f32[128,1,64,2,1,64]{0,5,4,3,2,1:T(8,128)}, u32[]{:S(2)}) copy-start(f32[128,1,64,2,1,64]{0,5,4,3,2,1:T(8,128)} %get-tuple-element.336) | copy-start | bytes 12582916 | tf_op jit(solution)/shard_map/while
  222.4 2.6 copy-start.1
  225.0 2.6 copy-start
  284.6 14.0 %copy-start.3 = (f32[45,8192]{1,0:T(8,128)S(1)}, f32[45,8192]{1,0:T(8,128)}, u32[]{:S(2)}) copy-start(f32[45,8192]{1,0:T(8,128)} %get-tuple-element.354) | copy-start | bytes 4423684 | tf_op jit(solution)/shard_map/while
  298.6 4.9 %copy-start.2 = (f32[128,1,64,2,1,64]{0,5,4,3,2,1:T(8,128)S(1)}, f32[128,1,64,2,1,64]{0,5,4,3,2,1:T(8,128)}, u32[]{:S(2)}) copy-start(f32[128,1,64,2,1,64]{0,5,4,3,2,1:T(8,128)} %get-tuple-element.336) | copy-start | bytes 12582916 | tf_op jit(solution)/shard_map/while
  303.4 2.6 copy-start.1
  306.1 2.6 copy-start
  365.7 14.0 %copy-start.3 = (f32[45,8192]{1,0:T(8,128)S(1)}, f32[45,8192]{1,0:T(8,128)}, u32[]{:S(2)}) copy-start(f32[45,8192]{1,0:T(8,128)} %get-tuple-element.354) | copy-start | bytes 4423684 | tf_op jit(solution)/shard_map/while
  379.6 4.9 %copy-start.2 = (f32[128,1,64,2,1,64]{0,5,4,3,2,1:T(8,128)S(1)}, f32[128,1,64,2,1,64]{0,5,4,3,2,1:T(8,128)}, u32[]{:S(2)}) copy-start(f32[128,1,64,2,1,64]{0,5,4,3,2,1:T(8,128)} %get-tuple-element.336) | copy-start | bytes 12582916 | tf_op jit(solution)/shard_map/while
  384.5 2.6 copy-start.1
  387.1 2.6 copy-start
  405.6 7.6 %collective-permute-start = (bf16[2,64,576]{1,2,0:T(8,128)(2,1)S(1)}, bf16[2,64,576]{1,2,0:T(8,128)(2,1)S(1)}, u32[]{:S(2)}, u32[]{:S(2)}) collective-permute-start(bf16[2,64,576]{1,2,0:T(8,128)(2,1)S(1)} %slice.187), channel_id=1, source_target_pairs={{0,8},{8,16},{16,24},{24,32},{32,40},{40,48},{48,56},{56,64},{64,7... | collective-permute-start | bytes 442376 | tf_op jit(solution)/shard_map/ppermute | solution.py:16
  420.4 2.2 collective-permute-start.1
where the time goes:
time: 431 us; the launch traced here: 424 us
  local copies, waits for them, and re-layouts  167 us (39%)
  matrix products  98.7 us (23%)
  other arithmetic  84 us (19%)
  waiting for transfers between devices  58.4 us (14%)
  starting transfers between devices  15.5 us (4%)
    convert_element_type x1, other arithmetic, aperture_screens(): real_part = (magnitude * jnp.cos(angles)).astype(jnp.bfloat16)  61.6 us
    dot_general x3, local copies, waits for them, and re-layouts, grid_patches(): jnp.einsum('grk,gkq->grq', stacked_rows, right_rows, preferred_element_ty...  52.8 us
    all_to_all x1, waiting for transfers between devices, shards(): lax.all_to_all(outgoing, ('tu', 'tv'), split_axis=0, concat_axis=0, tiled...  52.5 us
    dot_general x12, matrix products, grid_group(): placed = placed + jnp.dot(onehot, piece, precision=lax.Precision.HIGHEST)  41.2 us
    slice x3, local copies, waits for them, and re-layouts, grid_group(): piece = quarters[:, row_half, :, :, col_half, :].reshape(group_size, -1)  37.7 us
    dot_general x3, matrix products, grid_patches(): jnp.einsum('grk,gkq->grq', stacked_rows, right_rows, preferred_element_ty...  33 us
    reshape x3, local copies, waits for them, and re-layouts, grid_patches(): mixed.reshape(mixed.shape[0], 2 * mixed.shape[1], kernel_size)  22.2 us
    convert_element_type x3, local copies, waits for them, and re-layouts, grid_patches(): mixed = jnp.einsum('gpc,gcd->gpd', left_rows, operator_rows, preferred_el...  20.6 us
  transfers between devices with their start and end apart: 3, of which 3 were waited for; matrix products, arithmetic and copies ran while one was open for 0% of the time, Pallas kernels for 0%

commit v1 on v0

v1 whole, which is shorter than its diff:
```python
import functools
import math

import jax
import jax.numpy as jnp
import numpy as np
from jax import lax
from jax.experimental import pallas as pl
from jax.experimental.pallas import tpu as pltpu
from jax.sharding import PartitionSpec as P

SCREEN = 512
KSIZE = 64
PATCH = 128
PLANES = 4
SCREENS_DEV = 4
BLOCKS_DEV = 384
OWNERS = 128
TILE_U = 256
TILE_V = 512
POSITIONS = 32
GROUP = 4
MAX_GROUPS = BLOCKS_DEV // GROUP + POSITIONS
DEPTH = 8
EXT_U = TILE_U + KSIZE

SIN = (0.9999995827674866, -0.16666553914546967, 0.008332408033311367,
       -0.00019808740762528032, 2.6998227440344635e-06, -2.036623314438657e-08)
COS = (0.9999992251396179, -0.49999427795410156, 0.041659820824861526,
       -0.0013858915772289038, 2.4204400688176975e-05, -2.19788830690959e-07)


def sincos(x):
    z = x * x
    s = jnp.float32(SIN[-1])
    for c in SIN[-2::-1]:
        s = s * z + c
    k = jnp.float32(COS[-1])
    for c in COS[-2::-1]:
        k = k * z + c
    return s * x, k


def dft_rows():
    freq = np.arange(KSIZE) - KSIZE // 2
    turns = np.mod(freq[:, None] * np.arange(SCREEN)[None, :], SCREEN)
    angles = 2.0 * math.pi / SCREEN * turns
    return np.stack([np.cos(angles), -np.sin(angles)]).astype(np.float32)


def screen_kernel(w_ref, list_ref, amp_ref, phase_ref, f_ref, even_ref, odd_ref,
                  weight, parts, halves, kernels):
    coords = (lax.broadcasted_iota(jnp.int32, (1, SCREEN), 1) - SCREEN // 2).astype(jnp.float32)
    square = coords * coords * (1.0 / (SCREEN * SCREEN))
    for p in range(PLANES):
        turns = square * w_ref[p]
        turns = turns - jnp.floor(turns + 0.5)
        sin_p, cos_p = sincos(turns * (2.0 * math.pi))
        f_re, f_im = f_ref[0], f_ref[1]
        w_re = (f_re * cos_p - f_im * sin_p).astype(jnp.bfloat16)
        w_im = (f_re * sin_p + f_im * cos_p).astype(jnp.bfloat16)
        top = slice(p * 2 * KSIZE, p * 2 * KSIZE + KSIZE)
        low = slice(p * 2 * KSIZE + KSIZE, (p + 1) * 2 * KSIZE)
        weight[top, :SCREEN] = w_re
        weight[top, SCREEN:] = -w_im
        weight[low, :SCREEN] = w_im
        weight[low, SCREEN:] = w_re
    rows = 32
    for s in range(SCREENS_DEV):
        def fill(i, carry):
            at = pl.ds(pl.multiple_of(i * rows, rows), rows)
            sin_v, cos_v = sincos(phase_ref[s, at, :].astype(jnp.float32))
            amp = amp_ref[s, at, :].astype(jnp.float32)
            parts[s % 2, at, :] = (amp * cos_v).astype(jnp.bfloat16)
            parts[s % 2, pl.ds(pl.multiple_of(SCREEN + i * rows, rows), rows), :] = (
                amp * sin_v).astype(jnp.bfloat16)
            return carry
        lax.fori_loop(0, SCREEN // rows, fill, 0)
        for p in range(PLANES):
            half = jnp.dot(weight[p * 128:(p + 1) * 128, :], parts[s % 2],
                           preferred_element_type=jnp.float32).astype(jnp.bfloat16)
            halves[p, s * KSIZE:(s + 1) * KSIZE, :SCREEN] = half[:KSIZE]
            halves[p, s * KSIZE:(s + 1) * KSIZE, SCREEN:] = half[KSIZE:]
    for p in range(PLANES):
        out = lax.dot_general(halves[p], weight[p * 128:(p + 1) * 128, :],
                              (((1,), (1,)), ((), ())), preferred_element_type=jnp.float32)
        out = (out * (1.0 / SCREEN)).astype(jnp.bfloat16)
        for s in range(SCREENS_DEV):
            kernels[s * PLANES + p] = out[s * KSIZE:(s + 1) * KSIZE]

    def deliver(t, carry):
        even_ref[t] = kernels[list_ref[2 * t]]
        odd_ref[t] = kernels[list_ref[2 * t + 1]]
        return carry
    lax.fori_loop(0, OWNERS, deliver, 0)


def make_outgoing(depths, send_list, amp, phase):
    vmem = pl.BlockSpec(memory_space=pltpu.VMEM)
    smem = pl.BlockSpec(memory_space=pltpu.SMEM)
    slots = jax.ShapeDtypeStruct((OWNERS, KSIZE, 2 * KSIZE), jnp.bfloat16)
    return pl.pallas_call(
        screen_kernel,
        out_shape=(slots, slots),
        in_specs=[smem, smem, vmem, vmem, vmem],
        out_specs=(vmem, vmem),
        scratch_shapes=[
            pltpu.VMEM((PLANES * 128, 2 * SCREEN), jnp.bfloat16),
            pltpu.VMEM((2, 2 * SCREEN, SCREEN), jnp.bfloat16),
            pltpu.VMEM((PLANES, SCREENS_DEV * KSIZE, 2 * SCREEN), jnp.bfloat16),
            pltpu.VMEM((SCREENS_DEV * PLANES, KSIZE, 2 * KSIZE), jnp.bfloat16),
        ],
        compiler_params=pltpu.CompilerParams(vmem_limit_bytes=40 << 20),
        cost_estimate=pl.CostEstimate(flops=2_700_000_000, bytes_accessed=8_600_000,
                                      transcendentals=2_000_000),
        name="screens",
    )(depths, send_list.reshape(-1), amp, phase, jnp.asarray(dft_rows()))


def schedule_blocks(block_slot, block_pos, block_count):
    ids = jnp.arange(BLOCKS_DEV, dtype=jnp.int32)
    bins = (block_slot & 1) * POSITIONS + block_pos
    bins = jnp.where(ids < block_count[0], bins, -1)
    hot = (bins[:, None] == jnp.arange(2 * POSITIONS, dtype=jnp.int32)[None, :]).astype(jnp.float32)
    upto = (ids[:, None] >= ids[None, :]).astype(jnp.float32)
    rank = jnp.sum(jnp.dot(upto, hot, preferred_element_type=jnp.float32) * hot, axis=1) - 1.0
    groups = jnp.floor((jnp.sum(hot, axis=0) + (GROUP - 1.0)) * (1.0 / GROUP))
    b = jnp.arange(2 * POSITIONS, dtype=jnp.int32)
    before = (b[:, None] < b[None, :]) & (b[:, None] // POSITIONS == b[None, :] // POSITIONS)
    first = jnp.sum(jnp.where(before, groups[:, None], 0.0), axis=0)
    place = jnp.sum(hot * first[None, :], axis=1) * GROUP + rank
    place = place.astype(jnp.int32) + (block_slot & 1) * (MAX_GROUPS * GROUP)
    place = jnp.where(bins >= 0, place, -1)
    spots = jnp.arange(2 * MAX_GROUPS * GROUP, dtype=jnp.int32)
    code = ids * OWNERS + (block_slot >> 1) + 1
    codes = jnp.sum(jnp.where(place[None, :] == spots[:, None], code[None, :], 0), axis=1)
    last = (first + groups).astype(jnp.int32).reshape(2, 1, POSITIONS)
    anchors = jnp.sum((last <= jnp.arange(MAX_GROUPS, dtype=jnp.int32)[None, :, None]).astype(jnp.int32), axis=2)
    totals = jnp.sum(groups.reshape(2, POSITIONS), axis=1).astype(jnp.int32)
    return codes.reshape(2, -1), anchors, totals


def lanes_low(shape):
    return lax.broadcasted_iota(jnp.int32, shape, len(shape) - 1) < KSIZE


def operator_pair(first, second):
    zero = jnp.zeros((KSIZE, 2 * KSIZE), jnp.bfloat16)
    low = lanes_low((KSIZE, 2 * KSIZE))
    turned = [jnp.concatenate([v[:, KSIZE:], v[:, :KSIZE]], axis=1) for v in (first, second)]
    left = jnp.concatenate([
        jnp.where(low, first, zero), jnp.where(low, -turned[0], zero),
        jnp.where(low, zero, turned[1]), jnp.where(low, zero, -second)], axis=0)
    right = jnp.concatenate([
        jnp.where(low, turned[0], zero), jnp.where(low, first, zero),
        jnp.where(low, zero, second), jnp.where(low, zero, turned[1])], axis=0)
    return jnp.concatenate([left, right], axis=1)


def grid_groups(code_ref, anchor_ref, total_ref, recv, left_hbm, right_hbm, grid, lbuf, rbuf, sems):
    total = total_ref[0]

    def block_of(g, i):
        return jnp.maximum(code_ref[g * GROUP + i] - 1, 0)

    def copies(g, slot):
        out = []
        for i in range(GROUP):
            block = block_of(g, i) >> 7
            out.append(pltpu.make_async_copy(left_hbm.at[block], lbuf.at[slot, i], sems.at[slot, i]))
            out.append(pltpu.make_async_copy(
                right_hbm.at[block], rbuf.at[slot, pl.ds(i * KSIZE, KSIZE)], sems.at[slot, GROUP + i]))
        return out

    def start(g):
        for copy in copies(g, lax.rem(g, DEPTH)):
            copy.start()

    for g in range(DEPTH - 1):
        @pl.when(g < total)
        def _():
            start(g)

    def step(g, carry):
        slot = lax.rem(g, DEPTH)

        @pl.when(g + DEPTH - 1 < total)
        def _():
            start(g + DEPTH - 1)
        for copy in copies(g, slot):
            copy.wait()
        halves = []
        for pair in range(GROUP // 2):
            picked = []
            for i in (2 * pair, 2 * pair + 1):
                k = recv[block_of(g, i) & (OWNERS - 1)]
                used = code_ref[g * GROUP + i] > 0
                picked.append(jnp.where(used, k, jnp.zeros_like(k)))
            rows = jnp.concatenate([lbuf[slot, 2 * pair], lbuf[slot, 2 * pair + 1]], axis=1)
            mixed = jnp.dot(rows, operator_pair(*picked), preferred_element_type=jnp.float32)
            halves.append(mixed.astype(jnp.bfloat16))
        stacked = jnp.concatenate([
            jnp.concatenate([h[:, :PATCH] for h in halves], axis=1),
            jnp.concatenate([h[:, PATCH:] for h in halves], axis=1)], axis=0)
        patch = jnp.dot(stacked, rbuf[slot], preferred_element_type=jnp.float32)
        anchor = anchor_ref[g]
        row = pl.ds(pl.multiple_of((anchor >> 3) * KSIZE, KSIZE), PATCH)
        odd, col = anchor & 1, (anchor & 7) >> 1
        grid[odd, col, 0, row, :] += patch[:PATCH]
        grid[odd, col, 1, row, :] += patch[PATCH:]
        return carry
    lax.fori_loop(0, total, step, 0)


def first_kernel(code, anchor, total, recv, left, right, grid, lbuf, rbuf, sems):
    grid[...] = jnp.zeros_like(grid)
    grid_groups(code, anchor, total, recv, left, right, grid, lbuf, rbuf, sems)


def turn(v):
    return pltpu.roll(v, KSIZE, 1)


def second_kernel(code, anchor, total, recv, left, right, grid_in, main, bottom, side,
                  grid, lbuf, rbuf, sems):
    grid[...] = grid_in[...]
    grid_groups(code, anchor, total, recv, left, right, grid, lbuf, rbuf, sems)
    low = lanes_low((KSIZE, PATCH))
    for plane in range(2):
        for r in range(EXT_U // KSIZE):
            rows = slice(r * KSIZE, (r + 1) * KSIZE)
            shifted = [turn(grid[1, col, plane, rows, :]) for col in range(4)]
            for col in range(4):
                before = shifted[col - 1] if col else jnp.zeros_like(shifted[0])
                value = grid[0, col, plane, rows, :] + jnp.where(low, before, shifted[col])
                cols = slice(col * PATCH, (col + 1) * PATCH)
                if r < TILE_U // KSIZE:
                    main[plane, rows, cols] = value
                else:
                    bottom[plane, :, cols] = value.astype(jnp.bfloat16)
    for r in range(EXT_U // KSIZE):
        rows = slice(r * KSIZE, (r + 1) * KSIZE)
        value = jnp.where(low, turn(grid[1, 3, 0, rows, :]), grid[1, 3, 1, rows, :])
        side[rows, :] = value.astype(jnp.bfloat16)


GRID_SHAPE = (2, 4, 2, EXT_U, PATCH)


def grid_call(kernel, name, out_shape, code, anchor, total, recv, left, right, *more, scratch=()):
    vmem = pl.BlockSpec(memory_space=pltpu.VMEM)
    smem = pl.BlockSpec(memory_space=pltpu.SMEM)
    hbm = pl.BlockSpec(memory_space=pl.ANY)
    return pl.pallas_call(
        kernel,
        out_shape=out_shape,
        in_specs=[smem, smem, smem, vmem, hbm, hbm] + [vmem] * len(more),
        out_specs=jax.tree.map(lambda _: vmem, out_shape),
        scratch_shapes=[*scratch,
                        pltpu.VMEM((DEPTH, GROUP, PATCH, 2 * KSIZE), jnp.bfloat16),
                        pltpu.VMEM((DEPTH, GROUP * KSIZE, PATCH), jnp.bfloat16),
                        pltpu.SemaphoreType.DMA((DEPTH, 2 * GROUP))],
        compiler_params=pltpu.CompilerParams(vmem_limit_bytes=40 << 20),
        cost_estimate=pl.CostEstimate(flops=3_000_000_000, bytes_accessed=12_000_000,
                                      transcendentals=0),
        name=name,
    )(code, anchor, total, recv, left, right, *more)


def join_kernel(main, bottom, side, corner, out):
    low = lanes_low((TILE_U, PATCH))
    out[...] = main[...]
    out[:, :KSIZE, :] += bottom[...].astype(jnp.float32)
    edge = side[...].astype(jnp.float32)
    zero = jnp.zeros_like(edge)
    low_corner = lanes_low((KSIZE, PATCH))
    tip = corner[...].astype(jnp.float32)
    out[0, :, :PATCH] += jnp.where(low, edge, zero)
    out[1, :, :PATCH] += jnp.where(low, turn(edge), zero)
    out[0, :KSIZE, :PATCH] += jnp.where(low_corner, tip, zero[:KSIZE])
    out[1, :KSIZE, :PATCH] += jnp.where(low_corner, turn(tip), zero[:KSIZE])


def shards(aperture_amp, aperture_phase, plane_depths, send_list, send_count, vis_left, vis_right,
           block_slot, block_pos, block_count):
    axes = ("tu", "tv")
    n_tu, n_tv = lax.axis_size("tu"), lax.axis_size("tv")
    even, odd = make_outgoing(plane_depths, send_list, aperture_amp, aperture_phase)
    even = lax.all_to_all(even, axes, split_axis=0, concat_axis=0, tiled=True)
    odd = lax.all_to_all(odd, axes, split_axis=0, concat_axis=0, tiled=True)
    codes, anchors, totals = schedule_blocks(block_slot, block_pos, block_count)
    grid = grid_call(first_kernel, "grid_even", jax.ShapeDtypeStruct(GRID_SHAPE, jnp.float32),
                     codes[0], anchors[0], totals[:1], even, vis_left, vis_right)
    main, bottom, side = grid_call(
        second_kernel, "grid_odd",
        (jax.ShapeDtypeStruct((2, TILE_U, TILE_V), jnp.float32),
         jax.ShapeDtypeStruct((2, KSIZE, TILE_V), jnp.bfloat16),
         jax.ShapeDtypeStruct((EXT_U, PATCH), jnp.bfloat16)),
        codes[1], anchors[1], totals[1:], odd, vis_left, vis_right, grid,
        scratch=(pltpu.VMEM(GRID_SHAPE, jnp.float32),))
    bottom = lax.ppermute(bottom, "tu", [(i, i + 1) for i in range(n_tu - 1)])
    corner = lax.ppermute(side[TILE_U:], axes, [
        (u * n_tv + v, (u + 1) * n_tv + v + 1) for u in range(n_tu - 1) for v in range(n_tv - 1)])
    side = lax.ppermute(side[:TILE_U], "tv", [(i, i + 1) for i in range(n_tv - 1)])
    vmem = pl.BlockSpec(memory_space=pltpu.VMEM)
    return pl.pallas_call(
        join_kernel,
        out_shape=jax.ShapeDtypeStruct((2, TILE_U, TILE_V), jnp.float32),
        in_specs=[vmem] * 4,
        out_specs=vmem,
        compiler_params=pltpu.CompilerParams(vmem_limit_bytes=16 << 20),
        cost_estimate=pl.CostEstimate(flops=1_000_000, bytes_accessed=2_300_000, transcendentals=0),
        name="join_borders",
    )(main, bottom, side, corner)


def solution(mesh):
    placed = (
        P(("tu", "tv"), None, None),
        P(("tu", "tv"), None, None),
        P(),
        P(("tu", "tv"), None, None),
        P(("tu", "tv"), None),
        P(("tu", "tv"), None, None),
        P(("tu", "tv"), None, None),
        P(("tu", "tv")),
        P(("tu", "tv")),
        P(("tu", "tv")),
    )
    return jax.shard_map(
        shards, mesh=mesh, in_specs=placed, out_specs=P(None, "tu", "tv"), check_vma=False
    )
```

time: 431 us -> 163 us (0.38)
  the two profiles are of different devices: /device:TPU:0 before, /device:TPU:30 now
where the time goes in v1:
time: 163 us; the launch traced here: 160 us
  Pallas kernels  75 us (46%)
  starting transfers between devices  33.1 us (20%)
  waiting for transfers between devices  32.7 us (20%)
  local copies, waits for them, and re-layouts  17.6 us (11%)
    pallas_call x2, Pallas kernels, grid_call(): pl.pallas_call(kernel, out_shape=out_shape, in_specs=[smem, smem, smem, v...  64.6 us
    all_to_all x1, waiting for transfers between devices, shards(): even = lax.all_to_all(even, axes, split_axis=0, concat_axis=0, tiled=True)  26.6 us
    unnamed x25, local copies, waits for them, and re-layouts  16.7 us
    ppermute x1, starting transfers between devices, shards(): lax.ppermute(side[:TILE_U], 'tv', [(i, i + 1) for i in range(n_tv - 1)])  10.3 us
    all_to_all x1, starting transfers between devices, shards(): even = lax.all_to_all(even, axes, split_axis=0, concat_axis=0, tiled=True)  10.2 us
    pallas_call x1, Pallas kernels, make_outgoing(): pl.pallas_call(screen_kernel, out_shape=(slots, slots), in_specs=[smem, s...  9.32 us
    all_to_all x1, starting transfers between devices, shards(): odd = lax.all_to_all(odd, axes, split_axis=0, concat_axis=0, tiled=True)  8.74 us
    ppermute x1, waiting for transfers between devices, shards(): lax.ppermute(side[TILE_U:], axes, [(u * n_tv + v, (u + 1) * n_tv + v + 1)...  6.14 us
  transfers between devices with their start and end apart: 5, of which 2 were waited for; matrix products, arithmetic and copies ran while one was open for 1% of the time, Pallas kernels for 27%

profile of v1, /device:TPU:30, one launch (start us, length us, event | category | flops | bytes accessed | tf_op | source)
XLA Modules:
  0.0 160.3 jit_solution(15215026907563410080)
XLA Ops:
  0.0 0.8 copy.12
  0.8 0.1 reshape.112.list_ref
  0.9 0.0 copy-start.6
  0.9 1.6 copy-done.6
  2.5 0.0 copy-start.7
  2.5 1.6 copy-done.7
  4.1 0.0 copy-start.8
  4.1 0.7 copy-done.8
  4.8 0.0 copy-start.9
  4.8 0.9 copy-done.9
  5.7 9.3 %screens.1 = (bf16[128,64,128]{2,1,0:T(8,128)(2,1)S(1)}, bf16[128,64,128]{2,1,0:T(8,128)(2,1)S(1)}) custom-call(f32[4]{0:T(128)S(1)} %copy-done.8, s32[256]{0:T(256)S(1)} %reshape.112.list_ref, bf16[4,512,512]{2,1,0:T(8,128)(2,1)S(1)} %copy-done.6, bf16[4,512,512]{2,1,0:T(8,128)(2,1)S(1)} %copy-done.7, f32[2,64,512]{2,1,0:T(8,128)S(1)} %copy-done.9), custom_call_target="tpu_custom_call" | custom-call | flops 2700000000 | bytes 8600000 | tf_op jit(solution)/shard_map/screens/pallas_call | solution.py:102
  15.0 0.0 copy-start.4
  15.1 1.3 copy-done.4
  16.4 0.0 copy-start.5
  16.4 1.3 copy-done.5
  17.7 0.0 copy-start.10
  17.7 0.0 copy-start.11
  17.7 10.2 %all-to-all-start.1 = ((bf16[128,64,128]{2,1,0:T(8,128)(2,1)}), bf16[128,64,128]{2,1,0:T(8,128)(2,1)S(1)}, u32[]{:S(2)}, u32[]{:S(2)}) async-start(bf16[128,64,128]{2,1,0:T(8,128)(2,1)} %copy-done.5), calls=%async_computation.1 | async-start | bytes 4194304 | tf_op jit(solution)/shard_map/all_to_all | solution.py:289
  28.6 0.0 copy-done.10
  28.6 0.0 copy-done.11
  28.6 0.1 convert_reduce_fusion
  28.7 26.6 %all-to-all-done.1.recv = bf16[128,64,128]{2,1,0:T(8,128)(2,1)S(1)} async-done(((bf16[128,64,128]{2,1,0:T(8,128)(2,1)}), bf16[128,64,128]{2,1,0:T(8,128)(2,1)S(1)}, u32[]{:S(2)}, u32[]{:S(2)}) %all-to-all-start.1) | async-done | bytes 2097184 | tf_op jit(solution)/shard_map/all_to_all | solution.py:289
  55.3 0.0 copy-start.2
  55.3 1.3 copy-done.2
  56.6 8.7 %all-to-all-start = ((bf16[128,64,128]{2,1,0:T(8,128)(2,1)}), bf16[128,64,128]{2,1,0:T(8,128)(2,1)}, u32[]{:S(2)}, u32[]{:S(2)}) async-start(bf16[128,64,128]{2,1,0:T(8,128)(2,1)} %copy-done.4), calls=%async_computation | async-start | bytes 4194304 | tf_op jit(solution)/shard_map/all_to_all | solution.py:290
  65.4 0.1 floor.16
  65.5 0.1 select_reduce_fusion.2
  65.6 0.1 reduce_sum.70
  65.6 0.1 fusion.4
  65.8 0.7 fusion.5
  66.4 0.1 convert_reduce_fusion.1
  66.5 0.1 select_reduce_fusion.1
  66.6 0.2 fusion
  66.8 0.2 select_reduce_fusion
  67.1 0.0 copy-start
  67.1 2.8 %copy-done = bf16[384,64,128]{2,1,0:T(8,128)(2,1)S(1)} copy-done((bf16[384,64,128]{2,1,0:T(8,128)(2,1)S(1)}, bf16[384,64,128]{2,1,0:T(8,128)(2,1)}, u32[]{:S(2)}) %copy-start) | copy-done | bytes 6291480
  69.9 0.0 copy-start.3
  69.9 1.6 copy-done.3
  71.5 43.7 %grid_even.1.grid_in = f32[2,4,2,320,128]{4,3,2,1,0:T(8,128)S(1)} custom-call(s32[512]{0:T(512)S(1)} %get-tuple-element.15.code, s32[128]{0:T(128)S(1)} %get-tuple-element.19.anchor, s32[1]{0:T(128)} %get-tuple-element.23.total, bf16[128,64,128]{2,1,0:T(8,128)(2,1)S(1)} %copy-done.3, bf16[384,128,128]{2,1,0:T(8,128)(2,1)} %left.3, ...), custom_call_target="tpu_custom_call" | custom-call | flops 3000000000 | bytes 12000000 | tf_op jit(solution)/shard_map/grid_even/pallas_call | solution.py:254
  115.2 0.0 all-to-all-done.recv
  115.2 0.0 copy-start.1
  115.2 2.8 %copy-done.1 = bf16[384,64,128]{2,1,0:T(8,128)(2,1)S(1)} copy-done((bf16[384,64,128]{2,1,0:T(8,128)(2,1)S(1)}, bf16[384,64,128]{2,1,0:T(8,128)(2,1)}, u32[]{:S(2)}) %copy-start.1) | copy-done | bytes 6291480
  118.0 20.9 %grid_odd.1 = (f32[2,256,512]{2,1,0:T(8,128)S(1)}, bf16[2,64,512]{2,1,0:T(8,128)(2,1)S(1)}, bf16[320,128]{1,0:T(8,128)(2,1)S(1)}) custom-call(s32[512]{0:T(512)S(1)} %get-tuple-element.16.code, s32[128]{0:T(128)S(1)} %get-tuple-element.20.anchor, s32[1]{0:T(128)} %get-tuple-element.24.total, bf16[128,64,128]{2,1,0:T(8,128)(2,1)} %all-to-all-done.recv, ...), custom_call_target="tpu_custom_call" | custom-call | flops 3000000000 | bytes 12000000 | tf_op jit(solution)/shard_map/grid_odd/pallas_call | solution.py:254
  138.9 1.9 %collective-permute-start = (bf16[2,64,512]{2,1,0:T(8,128)(2,1)S(1)}, bf16[2,64,512]{2,1,0:T(8,128)(2,1)S(1)}, u32[]{:S(2)}, u32[]{:S(2)}) collective-permute-start(bf16[2,64,512]{2,1,0:T(8,128)(2,1)S(1)} %get-tuple-element.13), channel_id=1, source_target_pairs={{0,8},{8,16},{16,24},{24,32},{32,40},{40,48},{48,56},{56,64},{64,7... | collective-permute-start | bytes 393224 | tf_op jit(solution)/shard_map/ppermute | solution.py:301
  140.8 10.3 %collective-permute-start.1 = (bf16[256,128]{1,0:T(8,128)(2,1)S(1)}, bf16[256,128]{1,0:T(8,128)(2,1)S(1)}, u32[]{:S(2)}, u32[]{:S(2)}) collective-permute-start(bf16[256,128]{1,0:T(8,128)(2,1)S(1)} %slice.32), channel_id=1, source_target_pairs={{0,1},{1,2},{2,3},{3,4},{4,5},{5,6},{6,7},{8,9},{9,10},{10,11},{11... | collective-permute-start | bytes 196616 | tf_op jit(solution)/shard_map/ppermute | solution.py:304
  151.1 1.9 %collective-permute-start.2 = (bf16[64,128]{1,0:T(8,128)(2,1)S(1)}, bf16[64,128]{1,0:T(8,128)(2,1)S(1)}, u32[]{:S(2)}, u32[]{:S(2)}) collective-permute-start(bf16[64,128]{1,0:T(8,128)(2,1)S(1)} %slice.33), channel_id=1, source_target_pairs={{0,9},{1,10},{2,11},{3,12},{4,13},{5,14},{6,15},{8,17},{9,18},{10,... | collective-permute-start | bytes 49160 | tf_op jit(solution)/shard_map/ppermute | solution.py:302
  153.1 6.1 %collective-permute-done.2.corner = bf16[64,128]{1,0:T(8,128)(2,1)S(1)} collective-permute-done((bf16[64,128]{1,0:T(8,128)(2,1)S(1)}, bf16[64,128]{1,0:T(8,128)(2,1)S(1)}, u32[]{:S(2)}, u32[]{:S(2)}) %collective-permute-start.2) | collective-permute-done | bytes 16416 | tf_op jit(solution)/shard_map/ppermute | solution.py:302
  159.2 0.0 collective-permute-done.1.side
  159.2 0.0 collective-permute-done.bottom
  159.2 1.1 join_borders.1
  (9 shorter events, 0.1 us)
Async XLA Ops:
  0.9 1.6 copy-start.6
  2.5 1.6 copy-start.7
  4.1 0.7 copy-start.8
  4.8 0.9 copy-start.9
  15.0 1.3 copy-start.4
  16.4 1.3 copy-start.5
  17.7 10.9 %copy-start.10 = (s32[384]{0:T(512)S(1)}, s32[384]{0:T(512)}, u32[]{:S(2)}) copy-start(s32[384]{0:T(512)} %param.17) | copy-start | bytes 4612
  17.7 10.9 %copy-start.11 = (s32[384]{0:T(512)S(1)}, s32[384]{0:T(512)}, u32[]{:S(2)}) copy-start(s32[384]{0:T(512)} %param.18) | copy-start | bytes 4612
  17.7 37.6 %all-to-all-start.1 = ((bf16[128,64,128]{2,1,0:T(8,128)(2,1)}), bf16[128,64,128]{2,1,0:T(8,128)(2,1)S(1)}, u32[]{:S(2)}, u32[]{:S(2)}) async-start(bf16[128,64,128]{2,1,0:T(8,128)(2,1)} %copy-done.5), calls=%async_computation.1 | async-start | bytes 4194304 | tf_op jit(solution)/shard_map/all_to_all | solution.py:289
  55.3 1.3 copy-start.2
  56.6 58.6 %all-to-all-start = ((bf16[128,64,128]{2,1,0:T(8,128)(2,1)}), bf16[128,64,128]{2,1,0:T(8,128)(2,1)}, u32[]{:S(2)}, u32[]{:S(2)}) async-start(bf16[128,64,128]{2,1,0:T(8,128)(2,1)} %copy-done.4), calls=%async_computation | async-start | bytes 4194304 | tf_op jit(solution)/shard_map/all_to_all | solution.py:290
  67.1 2.8 %copy-start = (bf16[384,64,128]{2,1,0:T(8,128)(2,1)S(1)}, bf16[384,64,128]{2,1,0:T(8,128)(2,1)}, u32[]{:S(2)}) copy-start(bf16[384,64,128]{2,1,0:T(8,128)(2,1)} %right.3) | copy-start | bytes 18874372
  69.9 1.6 copy-start.3
  115.2 2.8 %copy-start.1 = (bf16[384,64,128]{2,1,0:T(8,128)(2,1)S(1)}, bf16[384,64,128]{2,1,0:T(8,128)(2,1)}, u32[]{:S(2)}) copy-start(bf16[384,64,128]{2,1,0:T(8,128)(2,1)} %right.3) | copy-start | bytes 18874372
  138.9 20.3 %collective-permute-start = (bf16[2,64,512]{2,1,0:T(8,128)(2,1)S(1)}, bf16[2,64,512]{2,1,0:T(8,128)(2,1)S(1)}, u32[]{:S(2)}, u32[]{:S(2)}) collective-permute-start(bf16[2,64,512]{2,1,0:T(8,128)(2,1)S(1)} %get-tuple-element.13), channel_id=1, source_target_pairs={{0,8},{8,16},{16,24},{24,32},{32,40},{40,48},{48,56},{56,64},{64,7... | collective-permute-start | bytes 393224 | tf_op jit(solution)/shard_map/ppermute | solution.py:301
  140.8 18.4 %collective-permute-start.1 = (bf16[256,128]{1,0:T(8,128)(2,1)S(1)}, bf16[256,128]{1,0:T(8,128)(2,1)S(1)}, u32[]{:S(2)}, u32[]{:S(2)}) collective-permute-start(bf16[256,128]{1,0:T(8,128)(2,1)S(1)} %slice.32), channel_id=1, source_target_pairs={{0,1},{1,2},{2,3},{3,4},{4,5},{5,6},{6,7},{8,9},{9,10},{10,11},{11... | collective-permute-start | bytes 196616 | tf_op jit(solution)/shard_map/ppermute | solution.py:304
  151.1 8.1 %collective-permute-start.2 = (bf16[64,128]{1,0:T(8,128)(2,1)S(1)}, bf16[64,128]{1,0:T(8,128)(2,1)S(1)}, u32[]{:S(2)}, u32[]{:S(2)}) collective-permute-start(bf16[64,128]{1,0:T(8,128)(2,1)S(1)} %slice.33), channel_id=1, source_target_pairs={{0,9},{1,10},{2,11},{3,12},{4,13},{5,14},{6,15},{8,17},{9,18},{10,... | collective-permute-start | bytes 49160 | tf_op jit(solution)/shard_map/ppermute | solution.py:302
